TPU v7x, 32 devices: a whole 2x2x4 slice. The times are simulated.
32 devices in a mesh: ctx: 8 (over z, x), seq: 2 (over y), tp: 2 (over core).
Axes of the slice: x: 2, y: 2, z: 4, core: 2. Of those that a mesh axis runs over, the one named last changes fastest.
Arguments:
- tokens: bfloat16 [4, 1024, 1024], P('seq', 'ctx'), may hold values from -6 to 6
- positions: int32 [4, 1024], P('seq', 'ctx'), may hold values from 0 to 1023, as said below
- attn_gain: float32 [1024], replicated, may hold values from 0.5 to 1.5
- ffn_gain: float32 [1024], replicated, may hold values from 0.5 to 1.5
- q_gain: float32 [64], replicated, may hold values from 0.5 to 1.5, as said below
- k_gain: float32 [64], replicated, may hold values from 0.5 to 1.5, as said below
- w_query: bfloat16 [1024, 1024], P(None, 'tp'), may hold values from -0.1875 to 0.1875
- w_key: bfloat16 [1024, 512], P(None, 'tp'), may hold values from -0.1875 to 0.1875
- w_value: bfloat16 [1024, 512], P(None, 'tp'), may hold values from -0.1875 to 0.1875
- w_out: bfloat16 [1024, 1024], P(None, 'tp'), may hold values from -1.5 to 1.5
- w_gate: bfloat16 [1024, 4608], P(None, 'tp'), may hold values from -0.1875 to 0.1875
- w_up: bfloat16 [1024, 4608], P(None, 'tp'), may hold values from -0.1875 to 0.1875
- w_down: bfloat16 [1024, 4608], P(None, 'tp'), may hold values from -0.09375 to 0.09375
- cotangent: bfloat16 [4, 1024, 1024], P('seq', 'ctx'), may hold values from -6 to 6
Outputs:
- layer_output: float32 [4, 1024, 1024], P('seq', 'ctx')
- input_grad: float32 [4, 1024, 1024], P('seq', 'ctx')
- wq_grad: float32 [1024, 1024], P(('ctx', 'seq'), 'tp')
- wk_grad: float32 [1024, 512], P(('ctx', 'seq'), 'tp')
- wv_grad: float32 [1024, 512], P(('ctx', 'seq'), 'tp')
- wo_grad: float32 [1024, 1024], P(('ctx', 'seq'), 'tp')
- wgate_grad: float32 [1024, 4608], P(('ctx', 'seq'), 'tp')
- wup_grad: float32 [1024, 4608], P(('ctx', 'seq'), 'tp')
- wdown_grad: float32 [1024, 4608], P(('ctx', 'seq'), 'tp')
- attngain_grad: float32 [1024], P(('ctx', 'seq'))
- ffngain_grad: float32 [1024], P(('ctx', 'seq'))
- qgain_grad: float32 [64], replicated
- kgain_grad: float32 [64], replicated
Inputs may be any that keep to these rules, and one draw needn't show every extreme that they name: positions[b, i] is i minus the first index of the document that holds token i of sequence b: 0 at a document's first token and at i = 0, else one more than at i - 1; sequence 0 is one document. `q_gain`: positive entries. `k_gain`: positive entries.
All inputs are finite; a program needn't handle non-finite values.
Results may differ from a plain program's by a relative error of at most 0.011.
Values may be sent and summed in bfloat16 or wider, within the bound.
No kernel may reach another device: no remote copies, remote signals or barrier semaphores. Data moves between devices by JAX's collectives and lax.ppermute only.
A program may use at most 192 MiB of HBM per device.

v0:
```python
import jax
import jax.numpy as jnp
from jax import lax
from jax.sharding import PartitionSpec as P

eps_norm = 1e-05
theta_base = 1000000.0
highest = lax.Precision.HIGHEST
negative = -1e30


def rms_stat(values):
    return lax.rsqrt(jnp.mean(values * values, axis=-1, keepdims=True) + eps_norm)


def rms_back(grad_in, values, stat_val):
    return stat_val * grad_in - values * stat_val**3 * jnp.mean(
        grad_in * values, axis=-1, keepdims=True
    )


def rope_tables(positions, head_dim):
    half_dim = head_dim // 2
    frequency = theta_base ** (-(jnp.arange(half_dim, dtype=jnp.float32) * 2.0) / head_dim)
    angles = positions.astype(jnp.float32)[..., None] * frequency
    return (jnp.cos(angles), jnp.sin(angles))


def rotate(values, cosine, sine_part):
    half_dim = values.shape[-1] // 2
    first_half = values[..., :half_dim]
    second_half = values[..., half_dim:]
    cos_full = cosine[..., None, :]
    sin_full = sine_part[..., None, :]
    return jnp.concatenate(
        [
            first_half * cos_full - second_half * sin_full,
            second_half * cos_full + first_half * sin_full,
        ],
        axis=-1,
    )


def unrotate(values, cosine, sine_part):
    half_dim = values.shape[-1] // 2
    first_half = values[..., :half_dim]
    second_half = values[..., half_dim:]
    cos_full = cosine[..., None, :]
    sin_full = sine_part[..., None, :]
    return jnp.concatenate(
        [
            first_half * cos_full + second_half * sin_full,
            second_half * cos_full - first_half * sin_full,
        ],
        axis=-1,
    )


def keep_carry(carry_in):
    return carry_in


def block_scores(query_grouped, key_piece, query_pos, lowest_pos, key_pos):
    head_dim = query_grouped.shape[-1]
    keys_split = key_piece.reshape(
        key_piece.shape[0], key_piece.shape[1], query_grouped.shape[2], head_dim
    )
    scores = jnp.einsum(
        "sqhgd,skhd->shgqk", query_grouped, keys_split, preferred_element_type=jnp.float32
    ) * head_dim ** (-0.5)
    allowed = (key_pos[None, None, :] <= query_pos[None, :, None]) & (
        key_pos[None, None, :] >= lowest_pos[:, :, None]
    )
    allowed = allowed[:, None, None, :, :]
    return (jnp.where(allowed, scores, negative), allowed, keys_split)


def block_grads(
    query_grouped,
    grad_grouped,
    log_sum,
    delta_stat,
    key_piece,
    value_piece,
    query_pos,
    lowest_pos,
    key_pos,
):
    scale_factor = query_grouped.shape[-1] ** (-0.5)
    scores, allowed, keys_split = block_scores(
        query_grouped, key_piece, query_pos, lowest_pos, key_pos
    )
    values_split = value_piece.reshape(keys_split.shape)
    probs = jnp.where(allowed, jnp.exp(scores - log_sum[..., None]), 0.0)
    grad_probs = jnp.einsum(
        "sqhgd,skhd->shgqk", grad_grouped, values_split, preferred_element_type=jnp.float32
    )
    grad_scores = probs * (grad_probs - delta_stat[..., None])
    query_grad = (
        jnp.einsum(
            "shgqk,skhd->sqhgd", grad_scores, keys_split.astype(jnp.float32), precision=highest
        )
        * scale_factor
    )
    key_grad = (
        jnp.einsum(
            "shgqk,sqhgd->skhd", grad_scores, query_grouped.astype(jnp.float32), precision=highest
        )
        * scale_factor
    )
    value_grad = jnp.einsum(
        "shgqk,sqhgd->skhd", probs, grad_grouped.astype(jnp.float32), precision=highest
    )
    return (query_grad, key_grad, value_grad)


def shards(
    tokens,
    positions,
    attn_gain,
    ffn_gain,
    q_gain,
    k_gain,
    w_query,
    w_key,
    w_value,
    w_out,
    w_gate,
    w_up,
    w_down,
    cotangent,
):
    seq_count, block_len, model_width = tokens.shape
    row_count = seq_count * block_len
    head_dim = q_gain.shape[0]
    q_heads = w_query.shape[1] // head_dim
    kv_heads = w_key.shape[1] // head_dim
    key_width = kv_heads * head_dim
    group_size = q_heads // kv_heads
    here_index = lax.axis_index("ctx")
    first_query = here_index * block_len
    last_query = first_query + block_len - 1
    query_index = first_query + jnp.arange(block_len, dtype=jnp.int32)
    lowest_key = query_index[None, :] - positions
    earliest = jnp.min(lowest_key)
    cosine, sine_part = rope_tables(positions, head_dim)
    flat_in = tokens.reshape(row_count, model_width).astype(jnp.float32)
    stat_one = rms_stat(flat_in)
    normed_one = (flat_in * stat_one * attn_gain).astype(jnp.bfloat16)
    query_raw = jnp.dot(normed_one, w_query, preferred_element_type=jnp.float32).reshape(
        seq_count, block_len, q_heads, head_dim
    )
    key_raw = jnp.dot(normed_one, w_key, preferred_element_type=jnp.float32).reshape(
        seq_count, block_len, kv_heads, head_dim
    )
    value_rows = (
        jnp.dot(normed_one, w_value, preferred_element_type=jnp.float32)
        .astype(jnp.bfloat16)
        .reshape(seq_count, block_len, key_width)
    )
    query_stat = rms_stat(query_raw)
    key_stat = rms_stat(key_raw)
    query_rot = rotate(query_raw * query_stat * q_gain, cosine, sine_part).astype(jnp.bfloat16)
    key_rot = rotate(key_raw * key_stat * k_gain, cosine, sine_part).astype(jnp.bfloat16)
    query_grouped = query_rot.reshape(seq_count, block_len, kv_heads, group_size, head_dim)
    key_rows = key_rot.reshape(seq_count, block_len, key_width)
    stats_shape = (seq_count, kv_heads, group_size, block_len)
    fold_start = (
        jnp.full(stats_shape, negative, jnp.float32),
        jnp.zeros(stats_shape, jnp.float32),
        jnp.zeros(stats_shape + (head_dim,), jnp.float32),
    )
    start_key = jnp.int32(0)
    key_piece = lax.all_gather(key_rows, "ctx", axis=1, tiled=True)
    value_piece = lax.all_gather(value_rows, "ctx", axis=1, tiled=True)
    piece_len = key_piece.shape[1]
    key_pos = jnp.arange(piece_len, dtype=jnp.int32)

    def attend_compute(carry_now):
        run_max, run_sum, run_acc = carry_now
        scores, allowed, keys_split = block_scores(
            query_grouped, key_piece, query_index, lowest_key, key_pos
        )
        new_max = jnp.maximum(run_max, jnp.max(scores, axis=-1))
        weights = jnp.where(allowed, jnp.exp(scores - new_max[..., None]), 0.0)
        values_split = value_piece.reshape(keys_split.shape).astype(jnp.float32)
        run_acc = jnp.einsum("shgqk,skhd->shgqd", weights, values_split, precision=highest)
        return (new_max, jnp.sum(weights, axis=-1), run_acc)

    visible = (start_key <= last_query) & (start_key + piece_len - 1 >= earliest)
    run_max, run_sum, run_acc = lax.cond(visible, attend_compute, keep_carry, fold_start)
    log_sum = run_max + jnp.log(run_sum)
    attended_heads = (run_acc / run_sum[..., None]).astype(jnp.bfloat16)
    attended_grouped = jnp.transpose(attended_heads, (0, 3, 1, 2, 4))
    attended = attended_grouped.reshape(row_count, q_heads * head_dim)
    attn_part = jnp.einsum("rq,dq->rd", attended, w_out, preferred_element_type=jnp.float32)
    mixed = flat_in + lax.psum(attn_part, "tp")
    stat_two = rms_stat(mixed)
    normed_two = (mixed * stat_two * ffn_gain).astype(jnp.bfloat16)
    gate_pre = jnp.dot(normed_two, w_gate, preferred_element_type=jnp.float32)
    up_pre = jnp.dot(normed_two, w_up, preferred_element_type=jnp.float32)
    sigmoid_val = jax.nn.sigmoid(gate_pre)
    silu_val = gate_pre * sigmoid_val
    hidden = (silu_val * up_pre).astype(jnp.bfloat16)
    ffn_part = jnp.einsum("rf,df->rd", hidden, w_down, preferred_element_type=jnp.float32)
    layer_output = mixed + lax.psum(ffn_part, "tp")
    cot_rows = cotangent.reshape(row_count, model_width)
    wdown_part = jnp.einsum("rd,rf->df", cot_rows, hidden, preferred_element_type=jnp.float32)
    grad_hidden = jnp.dot(cot_rows, w_down, preferred_element_type=jnp.float32)
    dsilu = sigmoid_val * (1.0 + gate_pre * (1.0 - sigmoid_val))
    grad_gate_pre = (grad_hidden * up_pre * dsilu).astype(jnp.bfloat16)
    grad_up_pre = (grad_hidden * silu_val).astype(jnp.bfloat16)
    wgate_part = jnp.einsum(
        "rd,rf->df", normed_two, grad_gate_pre, preferred_element_type=jnp.float32
    )
    wup_part = jnp.einsum("rd,rf->df", normed_two, grad_up_pre, preferred_element_type=jnp.float32)
    normed_part = jnp.einsum(
        "rf,df->rd", grad_gate_pre, w_gate, preferred_element_type=jnp.float32
    ) + jnp.einsum("rf,df->rd", grad_up_pre, w_up, preferred_element_type=jnp.float32)
    grad_normed_two = lax.psum(normed_part, "tp")
    ffngain_part = jnp.sum(grad_normed_two * mixed * stat_two, axis=0)
    grad_mixed = cot_rows.astype(jnp.float32) + rms_back(
        grad_normed_two * ffn_gain, mixed, stat_two
    )
    grad_mixed_bf = grad_mixed.astype(jnp.bfloat16)
    wout_part = jnp.einsum("rd,rq->dq", grad_mixed_bf, attended, preferred_element_type=jnp.float32)
    grad_attended = jnp.dot(grad_mixed_bf, w_out, preferred_element_type=jnp.float32).astype(
        jnp.bfloat16
    )
    grad_grouped = grad_attended.reshape(seq_count, block_len, kv_heads, group_size, head_dim)
    delta_rows = jnp.sum(
        grad_grouped.astype(jnp.float32) * attended_grouped.astype(jnp.float32), axis=-1
    )
    delta_stat = jnp.transpose(delta_rows, (0, 2, 3, 1))
    query_zero = jnp.zeros((seq_count, block_len, kv_heads, group_size, head_dim), jnp.float32)
    gathered_keys, gathered_values = (
        lax.all_gather(key_rows, "ctx", axis=1, tiled=True),
        lax.all_gather(value_rows, "ctx", axis=1, tiled=True),
    )
    seq_len = gathered_keys.shape[1]
    key_block = min(512, seq_len)
    block_total = seq_len // key_block
    full_zero = jnp.zeros((seq_count, seq_len, key_width), jnp.float32)

    def key_step(step_index, carry_in):
        start_key = step_index * key_block
        key_pos = start_key + jnp.arange(key_block, dtype=jnp.int32)

        def key_compute(carry_now):
            query_acc, key_acc, value_acc = carry_now
            key_piece = lax.dynamic_slice_in_dim(gathered_keys, start_key, key_block, 1)
            value_piece = lax.dynamic_slice_in_dim(gathered_values, start_key, key_block, 1)
            found_query, found_key, found_value = block_grads(
                query_grouped,
                grad_grouped,
                log_sum,
                delta_stat,
                key_piece,
                value_piece,
                query_index,
                lowest_key,
                key_pos,
            )
            key_old = lax.dynamic_slice_in_dim(key_acc, start_key, key_block, 1)
            value_old = lax.dynamic_slice_in_dim(value_acc, start_key, key_block, 1)
            key_acc = lax.dynamic_update_slice_in_dim(
                key_acc, key_old + found_key.reshape(seq_count, key_block, key_width), start_key, 1
            )
            value_acc = lax.dynamic_update_slice_in_dim(
                value_acc,
                value_old + found_value.reshape(seq_count, key_block, key_width),
                start_key,
                1,
            )
            return (query_acc + found_query, key_acc, value_acc)

        visible = (start_key <= last_query) & (start_key + key_block - 1 >= earliest)
        return lax.cond(visible, key_compute, keep_carry, carry_in)

    query_grad, key_grad_all, value_grad_all = lax.fori_loop(
        0, block_total, key_step, (query_zero, full_zero, full_zero)
    )
    key_grad_own, value_grad_own = (
        lax.psum_scatter(key_grad_all, "ctx", scatter_dimension=1, tiled=True),
        lax.psum_scatter(value_grad_all, "ctx", scatter_dimension=1, tiled=True),
    )
    query_grad_rot = query_grad.reshape(seq_count, block_len, q_heads, head_dim)
    key_grad_rot = key_grad_own.reshape(seq_count, block_len, kv_heads, head_dim)
    grad_query_norm = unrotate(query_grad_rot, cosine, sine_part)
    grad_key_norm = unrotate(key_grad_rot, cosine, sine_part)
    qgain_part = jnp.sum(grad_query_norm * query_raw * query_stat, axis=(0, 1, 2))
    kgain_part = jnp.sum(grad_key_norm * key_raw * key_stat, axis=(0, 1, 2))
    grad_query_raw = (
        rms_back(grad_query_norm * q_gain, query_raw, query_stat)
        .astype(jnp.bfloat16)
        .reshape(row_count, q_heads * head_dim)
    )
    grad_key_raw = (
        rms_back(grad_key_norm * k_gain, key_raw, key_stat)
        .astype(jnp.bfloat16)
        .reshape(row_count, key_width)
    )
    grad_value_raw = value_grad_own.astype(jnp.bfloat16).reshape(row_count, key_width)
    wq_part = jnp.einsum(
        "rd,rq->dq", normed_one, grad_query_raw, preferred_element_type=jnp.float32
    )
    wk_part = jnp.einsum("rd,rq->dq", normed_one, grad_key_raw, preferred_element_type=jnp.float32)
    wv_part = jnp.einsum(
        "rd,rq->dq", normed_one, grad_value_raw, preferred_element_type=jnp.float32
    )
    normed_part_one = jnp.einsum(
        "rq,dq->rd", grad_query_raw, w_query, preferred_element_type=jnp.float32
    )
    normed_part_one = normed_part_one + jnp.einsum(
        "rq,dq->rd", grad_key_raw, w_key, preferred_element_type=jnp.float32
    )
    normed_part_one = normed_part_one + jnp.einsum(
        "rq,dq->rd", grad_value_raw, w_value, preferred_element_type=jnp.float32
    )
    grad_normed_one = lax.psum(normed_part_one, "tp")
    attngain_part = jnp.sum(grad_normed_one * flat_in * stat_one, axis=0)
    input_grad = grad_mixed + rms_back(grad_normed_one * attn_gain, flat_in, stat_one)
    (
        wq_grad,
        wk_grad,
        wv_grad,
        wo_grad,
        wgate_grad,
        wup_grad,
        wdown_grad,
        attngain_grad,
        ffngain_grad,
    ) = (
        lax.psum_scatter(wq_part, ("ctx", "seq"), scatter_dimension=0, tiled=True),
        lax.psum_scatter(wk_part, ("ctx", "seq"), scatter_dimension=0, tiled=True),
        lax.psum_scatter(wv_part, ("ctx", "seq"), scatter_dimension=0, tiled=True),
        lax.psum_scatter(wout_part, ("ctx", "seq"), scatter_dimension=0, tiled=True),
        lax.psum_scatter(wgate_part, ("ctx", "seq"), scatter_dimension=0, tiled=True),
        lax.psum_scatter(wup_part, ("ctx", "seq"), scatter_dimension=0, tiled=True),
        lax.psum_scatter(wdown_part, ("ctx", "seq"), scatter_dimension=0, tiled=True),
        lax.psum_scatter(attngain_part, ("ctx", "seq"), scatter_dimension=0, tiled=True),
        lax.psum_scatter(ffngain_part, ("ctx", "seq"), scatter_dimension=0, tiled=True),
    )
    qgain_grad, kgain_grad = lax.psum((qgain_part, kgain_part), ("ctx", "seq", "tp"))
    return (
        layer_output.reshape(seq_count, block_len, model_width),
        input_grad.reshape(seq_count, block_len, model_width),
        wq_grad,
        wk_grad,
        wv_grad,
        wo_grad,
        wgate_grad,
        wup_grad,
        wdown_grad,
        attngain_grad,
        ffngain_grad,
        qgain_grad,
        kgain_grad,
    )


def solution(mesh):
    placed = (
        P("seq", "ctx", None),
        P("seq", "ctx"),
        P(),
        P(),
        P(),
        P(),
        P(None, "tp"),
        P(None, "tp"),
        P(None, "tp"),
        P(None, "tp"),
        P(None, "tp"),
        P(None, "tp"),
        P(None, "tp"),
        P("seq", "ctx", None),
    )
    return jax.shard_map(
        shards,
        mesh=mesh,
        in_specs=placed,
        out_specs=(
            P("seq", "ctx", None),
            P("seq", "ctx", None),
            P(("ctx", "seq"), "tp"),
            P(("ctx", "seq"), "tp"),
            P(("ctx", "seq"), "tp"),
            P(("ctx", "seq"), "tp"),
            P(("ctx", "seq"), "tp"),
            P(("ctx", "seq"), "tp"),
            P(("ctx", "seq"), "tp"),
            P(("ctx", "seq")),
            P(("ctx", "seq")),
            P(),
            P(),
        ),
        check_vma=False,
    )
```

profile of v0, /device:TPU:0, one launch (start us, length us, event | category | flops | bytes accessed | tf_op | source)
XLA Modules:
  0.0 1236.2 jit_solution(16476229728656146336)
XLA Ops:
  12.1 2.0 copy.76
  15.0 1.6 multiply_reduce_fusion.9
  20.2 1.7 multiply_reduce_fusion.6
  22.7 31.6 %all-gather.5.cloned.1.call-done = bf16[2,1024,256]{1,2,0:T(8,128)(2,1)} async-done(((bf16[2,128,256]{1,2,0:T(8,128)(2,1)}), bf16[2,1024,256]{1,2,0:T(8,128)(2,1)}) %all-gather.5.cloned.1.call-update) | async-done | bytes 1048592 | tf_op jit(solution)/shard_map/all_gather | solution.py:175
  54.3 41.1 %all-gather.3.cloned.1.call-done = bf16[2,1024,256]{1,2,0:T(8,128)(2,1)} async-done(((bf16[2,128,256]{1,2,0:T(8,128)(2,1)}), bf16[2,1024,256]{1,2,0:T(8,128)(2,1)}) %all-gather.3.cloned.1.call-update) | async-done | bytes 1048592 | tf_op jit(solution)/shard_map/all_gather | solution.py:174
  95.4 13.5 %conditional.2 = (f32[2,4,2,128]{3,2,1,0:T(2,128)}, f32[2,4,2,128]{3,2,1,0:T(2,128)}, f32[2,4,2,128,64]{3,4,2,1,0:T(8,128)S(1)}, f32[2,4,2,128]{3,2,1,0:T(2,128)S(1)}) conditional(s32[]{:T(128)} %convert_element_type.100, () %tuple.55, (s32[1024]{0:T(1024)S(1)}, s32[128]{0:T(128)S(1)}, s32[1024]{0:T(1024)S(1)}, s32[2,128]{1,0:T(2,128)S(1)}, ...), branch_computations={%region_4.0_spmd, %region_5.8_spmd} | conditional | flops 1904867328 | bytes 33629756 | solution.py:191
  95.9 2.8 fusion.2
  99.3 5.7 fusion.3
  104.9 3.3 fusion.4
  110.0 1.5 fusion.52
  111.5 12.6 %all-reduce.11.cloned.1.call-start = ((), (), s32[]{:S(2)}) async-start(), calls=%async_computation.12 | async-start | bytes 2097152 | tf_op jit(solution)/shard_map/psum | solution.py:220
  124.1 6.0 all-reduce.9.cloned.1.call-done
  132.4 4.0 fusion.70
  137.9 2.9 multiply_convert_fusion
  142.3 2.4 convolution_add_fusion.2
  145.5 20.0 %all-reduce.11.cloned.1.call-done = f32[256,1024]{1,0:T(8,128)} async-done(((f32[256,1024]{1,0:T(8,128)}), f32[256,1024]{1,0:T(8,128)}) %all-reduce.11.cloned.1.call-update) | async-done | bytes 1048592 | tf_op jit(solution)/shard_map/psum | solution.py:220
  165.5 1.5 multiply_reduce_fusion
  167.0 1.5 subtract_add_fusion
  173.5 1.6 broadcast_in_dim.61
  175.1 19.1 %while.22 = (s32[]{:T(128)}, f32[2,128,4,2,64]{1,4,3,2,0:T(8,128)}, f32[2,1024,256]{1,2,0:T(8,128)}, f32[2,1024,256]{1,2,0:T(8,128)S(1)}, s32[]{:T(128)}, /*inde...) while((s32[]{:T(128)}, f32[2,128,4,2,64]{1,4,3,2,0:T(8,128)}, ...), condition=%wide.region_17.18_spmd.clone, body=%wide.region_14.17_spmd.clone.sunk | while | flops 2696217088 | bytes 56661480 | solution.py:280
  175.8 17.7 %conditional.5 = ((f32[2,128,4,2,64]{1,4,3,2,0:T(8,128)}, f32[2,1024,256]{1,2,0:T(8,128)}, f32[2,1024,256]{1,2,0:T(8,128)S(1)})) conditional(s32[]{:T(128)} %convert_element_type.177, (f32[2,128,4,2,64]{1,4,3,2,0:T(8,128)}, f32[2,1024,256]{1,2,0:T(8,128)}, f32[2,1024,256]{1,2,0:T(8,128)S(1)}) %tuple.104, (s32[]{:T(128)}, ...), branch_computations={%region_15.15_spmd, %region_16.16_spmd} | conditional | flops 2696217088 | bytes 56658576 | solution.py:278
  179.1 4.1 fusion.17
  183.1 2.4 fusion.13
  185.6 3.7 fusion.26
  189.3 2.2 fusion.24
  194.3 1.8 copy.87
  196.4 5.2 fusion.71
  204.4 77.8 %reduce-scatter.12.cloned.1.call-done = f32[2,128,256]{1,2,0:T(8,128)} async-done(((f32[2,1024,256]{1,2,0:T(8,128)}), f32[2,128,256]{1,2,0:T(8,128)}) %reduce-scatter.12.cloned.1.call-update) | async-done | bytes 262160 | tf_op jit(solution)/shard_map/reduce_scatter | solution.py:284
  284.1 1.5 convolution_add_fusion.1
  285.6 67.4 %reduce-scatter.14.cloned.1.call-done = f32[2,128,256]{2,1,0:T(8,128)} async-done(((f32[2,1024,256]{2,1,0:T(8,128)}), f32[2,128,256]{2,1,0:T(8,128)}) %reduce-scatter.14.cloned.1.call-update) | async-done | bytes 262160 | tf_op jit(solution)/shard_map/reduce_scatter | solution.py:285
  354.0 2.3 convolution_add_fusion
  356.5 1.8 fusion.50
  358.4 1.9 fusion.46
  363.2 5.0 convolution_bitcast_fusion.1
  368.2 9.9 copy.102
  379.6 5.1 fusion.74
  385.9 5.1 fusion.73
  392.9 41.8 %all-reduce.2 = (f32[64]{0:T(128)}, f32[64]{0:T(128)}) all-reduce(f32[64]{0:T(128)S(1)} %copy-done.38, f32[64]{0:T(128)S(1)} %copy-done.39), channel_id=1, replica_groups=mesh['ctx'=8,'seq'=2,'tp'=2] {'ctx','seq','tp'}, use_global_device_ids=true, to_apply=%region_36.37 | all-reduce | flops 128 | bytes 1024 | tf_op jit(solution)/shard_map/psum | solution.py:344
  434.8 2.4 add.233
  437.2 1.5 fusion.41
  438.8 40.1 %all-reduce.3 = (f32[1024]{0:T(1024)S(1)}, f32[1024]{0:T(1024)S(1)}) all-reduce(f32[1024]{0:T(1024)S(1)} %get-tuple-element.700, f32[1024]{0:T(1024)S(1)} %get-tuple-element.698), channel_id=11, replica_groups=mesh['ctx'=8,'seq'=2,'tp'=2] {'ctx','seq'}, use_global_device_ids=true, to_apply=%region_32.33.clone | all-reduce | flops 2048 | bytes 16384
  480.1 2.8 fusion.38
  482.9 60.9 %reduce-scatter.16.cloned.1.call-done = f32[64,512]{1,0:T(8,128)} async-done(((f32[1024,512]{1,0:T(8,128)}), f32[64,512]{1,0:T(8,128)}) %reduce-scatter.16.cloned.1.call-update) | async-done | bytes 131088 | tf_op jit(solution)/shard_map/reduce_scatter | solution.py:334
  543.8 78.8 %reduce-scatter.18.cloned.1.call-done = f32[64,256]{1,0:T(8,128)} async-done(((f32[1024,256]{1,0:T(8,128)}), f32[64,256]{1,0:T(8,128)}) %reduce-scatter.18.cloned.1.call-update) | async-done | bytes 65552 | tf_op jit(solution)/shard_map/reduce_scatter | solution.py:335
  622.6 77.9 %reduce-scatter.20.cloned.1.call-done = f32[64,256]{1,0:T(8,128)} async-done(((f32[1024,256]{1,0:T(8,128)}), f32[64,256]{1,0:T(8,128)}) %reduce-scatter.20.cloned.1.call-update) | async-done | bytes 65552 | tf_op jit(solution)/shard_map/reduce_scatter | solution.py:336
  700.5 174.1 %reduce-scatter.28.cloned.1.call-done = f32[64,2304]{1,0:T(8,128)} async-done(((f32[1024,2304]{1,0:T(8,128)}), f32[64,2304]{1,0:T(8,128)}) %reduce-scatter.28.cloned.1.call-update) | async-done | bytes 589840
  874.6 177.6 %reduce-scatter.26.cloned.1.call-done = f32[64,2304]{1,0:T(8,128)} async-done(((f32[1024,2304]{1,0:T(8,128)}), f32[64,2304]{1,0:T(8,128)}) %reduce-scatter.26.cloned.1.call-update) | async-done | bytes 589840 | tf_op jit(solution)/shard_map/reduce_scatter | solution.py:339
  1052.2 177.1 %reduce-scatter.24.cloned.1.call-done = f32[64,2304]{1,0:T(8,128)} async-done(((f32[1024,2304]{1,0:T(8,128)}), f32[64,2304]{1,0:T(8,128)}) %reduce-scatter.24.cloned.1.call-update) | async-done | bytes 589840 | tf_op jit(solution)/shard_map/reduce_scatter | solution.py:338
  (197 shorter events, 42.1 us)
Async XLA Ops:
  7.2 102.8 %copy-start = (bf16[1024,512]{1,0:T(8,128)(2,1)S(1)}, bf16[1024,512]{1,0:T(8,128)(2,1)}, u32[]{:S(2)}) copy-start(bf16[1024,512]{1,0:T(8,128)(2,1)} %param.29) | copy-start | bytes 3145732
  7.2 7.6 copy-start.6
  7.2 7.6 copy-start.33
  7.2 7.0 copy-start.37
  7.2 10.1 copy-start.36
  7.2 11.6 copy-start.19
  7.3 47.1 %all-gather.5.cloned.1.call-start = ((), (), s32[]{:S(2)}) async-start(), calls=%async_computation.10 | async-start | bytes 1179648 | tf_op jit(solution)/shard_map/all_gather | solution.py:175
  12.1 83.3 %all-gather.3.cloned.1.call-start = ((), (), s32[]{:S(2)}) async-start(), calls=%async_computation.9 | async-start | bytes 1179648 | tf_op jit(solution)/shard_map/all_gather | solution.py:174
  15.0 7.1 copy-start.10
  15.0 6.9 copy-start.35
  18.2 111.9 %all-reduce.9.cloned.1.call-start = ((), (), s32[]{:S(2)}) async-start(), calls=%async_computation.11 | async-start | bytes 2097152 | tf_op jit(solution)/shard_map/psum | solution.py:197
  95.9 3.4 copy-start.12
  108.9 23.3 %copy-start.34 = (f32[1024]{0:T(1024)S(1)}, f32[1024]{0:T(1024)}, u32[]{:S(2)}) copy-start(f32[1024]{0:T(1024)} %param.23) | copy-start | bytes 12292
  110.0 14.1 %copy-start.21 = (bf16[2,128,4,2,64]{1,0,4,3,2:T(2,128)(2,1)}, bf16[2,128,4,2,64]{1,0,4,3,2:T(2,128)(2,1)S(1)}, u32[]{:S(2)}) copy-start(bf16[2,128,4,2,64]{1,0,4,3,2:T(2,128)(2,1)S(1)} %copy.79) | copy-start | bytes 786436
  111.5 54.0 %all-reduce.11.cloned.1.call-start = ((), (), s32[]{:S(2)}) async-start(), calls=%async_computation.12 | async-start | bytes 2097152 | tf_op jit(solution)/shard_map/psum | solution.py:220
  131.6 35.4 %copy-start.4 = (f32[256,1024]{1,0:T(8,128)}, f32[256,1024]{1,0:T(8,128)S(1)}, u32[]{:S(2)}) copy-start(f32[256,1024]{1,0:T(8,128)S(1)} %get-tuple-element.741) | copy-start | bytes 3145732
  132.2 4.2 slice-start
  132.3 4.1 copy-start.13
  132.4 4.1 slice-start.1
  132.4 5.5 slice-start.4
  136.5 5.8 slice-start.2
  137.9 4.4 slice-start.3
  142.3 24.7 %copy-start.26 = (bf16[2,128,1024]{2,1,0:T(8,128)(2,1)S(1)}, bf16[2,128,1024]{2,1,0:T(8,128)(2,1)}, u32[]{:S(2)}) copy-start(bf16[2,128,1024]{2,1,0:T(8,128)(2,1)} %param.33) | copy-start | bytes 1572868
  144.7 137.5 %reduce-scatter.12.cloned.1.call-start = ((), (), s32[]{:S(2)}) async-start(), calls=%async_computation.13 | async-start | bytes 2359296 | tf_op jit(solution)/shard_map/reduce_scatter | solution.py:284
  185.6 5.9 copy-start.2
  194.2 158.8 %reduce-scatter.14.cloned.1.call-start = ((), (), s32[]{:S(2)}) async-start(), calls=%async_computation.14 | async-start | bytes 2359296 | tf_op jit(solution)/shard_map/reduce_scatter | solution.py:285
  196.2 238.6 %all-reduce.13.cloned.1.call-start = ((), (), s32[]{:S(2)}) async-start(), calls=%async_computation.22 | async-start | bytes 4194304 | tf_op jit(solution)/shard_map/psum | solution.py:206
  196.4 6.4 copy-start.16
  196.4 7.5 copy-start.20
  201.6 81.6 %copy-start.18 = (f32[2,128,4,64]{1,3,2,0:T(8,128)S(1)}, f32[2,128,4,64]{1,3,2,0:T(8,128)}, u32[]{:S(2)}) copy-start(f32[2,128,4,64]{1,3,2,0:T(8,128)} %copy-done.17) | copy-start | bytes 786436
  203.9 80.2 %copy-start.23 = (bf16[2,128,8,64]{1,0,3,2:T(2,128)(2,1)}, bf16[2,128,8,64]{1,0,3,2:T(2,128)(2,1)S(1)}, u32[]{:S(2)}) copy-start(bf16[2,128,8,64]{1,0,3,2:T(2,128)(2,1)S(1)} %copy.85) | copy-start | bytes 786436
  284.0 72.5 %copy-start.9 = (f32[256,1024]{1,0:T(8,128)S(1)}, f32[256,1024]{1,0:T(8,128)}, u32[]{:S(2)}) copy-start(f32[256,1024]{1,0:T(8,128)} %copy-done.8) | copy-start | bytes 3145732
  284.0 72.5 %copy-start.22 = (bf16[2,128,4,2,64]{1,0,4,3,2:T(2,128)(2,1)S(1)}, bf16[2,128,4,2,64]{1,0,4,3,2:T(2,128)(2,1)}, u32[]{:S(2)}) copy-start(bf16[2,128,4,2,64]{1,0,4,3,2:T(2,128)(2,1)} %copy-done.21) | copy-start | bytes 786436
  356.4 2.0 copy-start.11
  356.4 2.0 copy-start.24
  356.4 126.5 %reduce-scatter.22.cloned.1.call-start = ((), (), s32[]{:S(2)}) async-start(), calls=%async_computation.18 | async-start | bytes 2228224 | tf_op jit(solution)/shard_map/reduce_scatter | solution.py:337
  358.3 185.5 %reduce-scatter.16.cloned.1.call-start = ((), (), s32[]{:S(2)}) async-start(), calls=%async_computation.15 | async-start | bytes 2228224 | tf_op jit(solution)/shard_map/reduce_scatter | solution.py:334
  360.3 2.9 copy-start.27
  360.3 2.9 copy-start.28
  360.3 262.3 %reduce-scatter.18.cloned.1.call-start = ((), (), s32[]{:S(2)}) async-start(), calls=%async_computation.16 | async-start | bytes 1114112 | tf_op jit(solution)/shard_map/reduce_scatter | solution.py:335
  361.7 338.8 %reduce-scatter.20.cloned.1.call-start = ((), (), s32[]{:S(2)}) async-start(), calls=%async_computation.17 | async-start | bytes 1114112 | tf_op jit(solution)/shard_map/reduce_scatter | solution.py:336
  363.1 511.5 %reduce-scatter.28.cloned.1.call-start = ((), (), s32[]{:S(2)}) async-start(), calls=%async_computation.21 | async-start | bytes 10027008
  378.2 674.0 %reduce-scatter.26.cloned.1.call-start = ((), (), s32[]{:S(2)}) async-start(), calls=%async_computation.20 | async-start | bytes 10027008 | tf_op jit(solution)/shard_map/reduce_scatter | solution.py:339
  384.7 844.6 %reduce-scatter.24.cloned.1.call-start = ((), (), s32[]{:S(2)}) async-start(), calls=%async_computation.19 | async-start | bytes 10027008 | tf_op jit(solution)/shard_map/reduce_scatter | solution.py:338
  391.0 1.9 copy-start.39
  391.0 43.8 %copy-start.5 = (f32[256,1024]{1,0:T(8,128)S(1)}, f32[256,1024]{1,0:T(8,128)}, u32[]{:S(2)}) copy-start(f32[256,1024]{1,0:T(8,128)} %copy-done.4) | copy-start | bytes 3145732
  391.0 46.2 %copy-start.7 = (bf16[2,128,1024]{2,1,0:T(8,128)(2,1)S(1)}, bf16[2,128,1024]{2,1,0:T(8,128)(2,1)}, u32[]{:S(2)}) copy-start(bf16[2,128,1024]{2,1,0:T(8,128)(2,1)} %param.20) | copy-start | bytes 1572868
  434.8 794.5 %copy-start.1 = (bf16[1024,512]{1,0:T(8,128)(2,1)S(1)}, bf16[1024,512]{1,0:T(8,128)(2,1)}, u32[]{:S(2)}) copy-start(bf16[1024,512]{1,0:T(8,128)(2,1)} %param.29) | copy-start | bytes 3145732
  (13 other events, 15.9 us)
Sparse Core Ops, SparseCore 0:
  12.2 42.1 all-gather.4
  56.9 38.3 all-gather.2
  111.6 18.4 all-reduce.8
  144.8 20.5 all-reduce.10
  194.4 87.7 reduce-scatter.11
  285.6 67.4 reduce-scatter.13
  356.5 20.3 all-reduce.12
  379.8 82.7 reduce-scatter.21
  465.5 78.2 reduce-scatter.15
  546.4 76.0 reduce-scatter.17
  625.4 75.0 reduce-scatter.19
  706.6 167.9 reduce-scatter.27
  880.8 171.3 reduce-scatter.25
  1058.3 170.8 reduce-scatter.23
where the time goes:
time: 1250 us; the launch traced here: 1240 us
  waiting for transfers between devices  990 us (79%)
  blocking collectives  82 us (7%)
  matrix products  71.3 us (6%)
  local copies, waits for them, and re-layouts  31.9 us (3%)
  other arithmetic  29.3 us (2%)
  between operations  16.4 us (1%)
  starting transfers between devices  13.3 us (1%)
    reduce_scatter x1, waiting for transfers between devices, shards(): lax.psum_scatter(wup_part, ('ctx', 'seq'), scatter_dimension=0, tiled=True)  178 us
    reduce_scatter x1, waiting for transfers between devices, shards(): lax.psum_scatter(wgate_part, ('ctx', 'seq'), scatter_dimension=0, tiled=T...  177 us
    unnamed x15, waiting for transfers between devices  174 us
    reduce_scatter x1, waiting for transfers between devices, shards(): lax.psum_scatter(wk_part, ('ctx', 'seq'), scatter_dimension=0, tiled=True)  78.8 us
    reduce_scatter x1, waiting for transfers between devices, shards(): lax.psum_scatter(wv_part, ('ctx', 'seq'), scatter_dimension=0, tiled=True)  77.9 us
    reduce_scatter x1, waiting for transfers between devices, shards(): lax.psum_scatter(key_grad_all, 'ctx', scatter_dimension=1, tiled=True)  77.8 us
    reduce_scatter x1, waiting for transfers between devices, shards(): lax.psum_scatter(value_grad_all, 'ctx', scatter_dimension=1, tiled=True)  67.4 us
    reduce_scatter x1, waiting for transfers between devices, shards(): lax.psum_scatter(wq_part, ('ctx', 'seq'), scatter_dimension=0, tiled=True)  60.9 us
  transfers between devices with their start and end apart: 14, of which 12 were waited for; matrix products, arithmetic and copies ran while one was open for 5% of the time, Pallas kernels for 0%

commit v1 on v0

--- a/solution.py
+++ b/solution.py
@@ -171,8 +171,11 @@
         jnp.zeros(stats_shape + (head_dim,), jnp.float32),
     )
     start_key = jnp.int32(0)
-    key_piece = lax.all_gather(key_rows, "ctx", axis=1, tiled=True)
-    value_piece = lax.all_gather(value_rows, "ctx", axis=1, tiled=True)
+    key_piece, value_piece = jnp.split(
+        lax.all_gather(jnp.concatenate([key_rows, value_rows], axis=0), "ctx", axis=1, tiled=True),
+        [key_rows.shape[0]],
+        axis=0,
+    )
     piece_len = key_piece.shape[1]
     key_pos = jnp.arange(piece_len, dtype=jnp.int32)
 

time: 1250 us -> 1290 us (1.032)
  waiting for transfers between devices: 990 us -> 1040 us
    all_gather x2 -> x3, waiting for transfers between devices: 72.6 us -> 125 us  [the longest x1 48.6 us: shards(): lax.all_gather(jnp.concatenate([key_rows, value_rows], axis=0), 'ctx', ax...]
    unnamed x15 -> x16, waiting for transfers between devices: 174 us -> 176 us
  transfers between devices with their start and end apart: 14 -> 15, of which waited for: 12 -> 13; matrix products, arithmetic and copies ran while one was open for 5% -> 5% of each run, Pallas kernels for 0% -> 0%
where the time goes in v1:
time: 1290 us; the launch traced here: 1280 us
  waiting for transfers between devices  1040 us (81%)
  blocking collectives  82.3 us (6%)
  matrix products  69.2 us (5%)
  local copies, waits for them, and re-layouts  31.8 us (2%)
  other arithmetic  30.6 us (2%)
  between operations  16.6 us (1%)
  starting transfers between devices  13.4 us (1%)
    reduce_scatter x1, waiting for transfers between devices, shards(): lax.psum_scatter(wgate_part, ('ctx', 'seq'), scatter_dimension=0, tiled=T...  177 us
    reduce_scatter x1, waiting for transfers between devices, shards(): lax.psum_scatter(wup_part, ('ctx', 'seq'), scatter_dimension=0, tiled=True)  177 us
    unnamed x16, waiting for transfers between devices  176 us
    reduce_scatter x1, waiting for transfers between devices, shards(): lax.psum_scatter(wk_part, ('ctx', 'seq'), scatter_dimension=0, tiled=True)  78.6 us
    reduce_scatter x1, waiting for transfers between devices, shards(): lax.psum_scatter(wv_part, ('ctx', 'seq'), scatter_dimension=0, tiled=True)  77.7 us
    reduce_scatter x1, waiting for transfers between devices, shards(): lax.psum_scatter(key_grad_all, 'ctx', scatter_dimension=1, tiled=True)  75.5 us
    reduce_scatter x1, waiting for transfers between devices, shards(): lax.psum_scatter(value_grad_all, 'ctx', scatter_dimension=1, tiled=True)  67.3 us
    reduce_scatter x1, waiting for transfers between devices, shards(): lax.psum_scatter(wq_part, ('ctx', 'seq'), scatter_dimension=0, tiled=True)  60.7 us
  transfers between devices with their start and end apart: 15, of which 13 were waited for; matrix products, arithmetic and copies ran while one was open for 5% of the time, Pallas kernels for 0%

profile of v1, /device:TPU:0, one launch (start us, length us, event | category | flops | bytes accessed | tf_op | source)
XLA Modules:
  0.0 1283.9 jit_solution(14833113642187499505)
XLA Ops:
  18.4 1.7 multiply_reduce_fusion.6
  21.0 48.6 %all-gather.4.cloned.1.call-done = bf16[4,1024,256]{1,2,0:T(8,128)(2,1)} async-done(((bf16[4,128,256]{1,2,0:T(8,128)(2,1)}), bf16[4,1024,256]{1,2,0:T(8,128)(2,1)}) %all-gather.4.cloned.1.call-update) | async-done | bytes 2097168 | tf_op jit(solution)/shard_map/all_gather | solution.py:175
  69.6 13.9 %conditional.2 = (f32[2,4,2,128]{3,2,1,0:T(2,128)}, f32[2,4,2,128]{3,2,1,0:T(2,128)}, f32[2,4,2,128,64]{3,4,2,1,0:T(8,128)S(1)}, f32[2,4,2,128]{3,2,1,0:T(2,128)S(1)}) conditional(s32[]{:T(128)} %convert_element_type.100, () %tuple.55, (s32[1024]{0:T(1024)S(1)}, s32[128]{0:T(128)S(1)}, s32[1024]{0:T(1024)S(1)}, s32[2,128]{1,0:T(2,128)S(1)}, ...), branch_computations={%region_4.0_spmd, %region_5.8_spmd} | conditional | flops 1904867328 | bytes 33629728 | solution.py:194
  70.1 1.7 fusion.68
  71.8 1.5 fusion.2
  73.9 5.7 fusion.3
  79.5 3.3 fusion.4
  84.7 1.5 fusion.52
  86.2 12.7 all-reduce.11.cloned.1.call-start
  98.9 5.1 all-reduce.9.cloned.1.call-done
  105.6 4.4 fusion.71
  111.6 2.9 multiply_convert_fusion
  116.0 2.4 convolution_add_fusion.2
  120.3 18.8 %all-reduce.11.cloned.1.call-done = f32[256,1024]{1,0:T(8,128)} async-done(((f32[256,1024]{1,0:T(8,128)}), f32[256,1024]{1,0:T(8,128)}) %all-reduce.11.cloned.1.call-update) | async-done | bytes 1048592 | tf_op jit(solution)/shard_map/psum | solution.py:223
  139.1 2.1 multiply_reduce_fusion
  141.2 1.5 subtract_add_fusion
  146.6 35.6 %all-gather.8.cloned.1.call-done = bf16[2,1024,256]{1,2,0:T(8,128)(2,1)} async-done(((bf16[2,128,256]{1,2,0:T(8,128)(2,1)}), bf16[2,1024,256]{1,2,0:T(8,128)(2,1)}) %all-gather.8.cloned.1.call-update) | async-done | bytes 1048592 | tf_op jit(solution)/shard_map/all_gather | solution.py:241
  182.2 40.9 %all-gather.6.cloned.1.call-done = bf16[2,1024,256]{1,2,0:T(8,128)(2,1)} async-done(((bf16[2,128,256]{1,2,0:T(8,128)(2,1)}), bf16[2,1024,256]{1,2,0:T(8,128)(2,1)}) %all-gather.6.cloned.1.call-update) | async-done | bytes 1048592 | tf_op jit(solution)/shard_map/all_gather | solution.py:240
  224.2 1.6 broadcast_in_dim.61
  225.8 19.1 %while.22 = (s32[]{:T(128)}, f32[2,128,4,2,64]{1,4,3,2,0:T(8,128)}, f32[2,1024,256]{1,2,0:T(8,128)}, f32[2,1024,256]{1,2,0:T(8,128)S(1)}, s32[]{:T(128)}, /*inde...) while((s32[]{:T(128)}, f32[2,128,4,2,64]{1,4,3,2,0:T(8,128)}, ...), condition=%wide.region_17.18_spmd.clone, body=%wide.region_14.17_spmd.clone.sunk | while | flops 2696217088 | bytes 56661480 | solution.py:283
  226.5 17.8 %conditional.5 = ((f32[2,128,4,2,64]{1,4,3,2,0:T(8,128)}, f32[2,1024,256]{1,2,0:T(8,128)}, f32[2,1024,256]{1,2,0:T(8,128)S(1)})) conditional(s32[]{:T(128)} %convert_element_type.177, (f32[2,128,4,2,64]{1,4,3,2,0:T(8,128)}, f32[2,1024,256]{1,2,0:T(8,128)}, f32[2,1024,256]{1,2,0:T(8,128)S(1)}) %tuple.105, (s32[]{:T(128)}, ...), branch_computations={%region_15.15_spmd, %region_16.16_spmd} | conditional | flops 2696217088 | bytes 56658576 | solution.py:281
  229.8 4.1 fusion.17
  233.9 2.4 fusion.13
  236.3 3.7 fusion.26
  240.0 2.2 fusion.24
  245.0 1.8 copy.91
  247.2 5.2 fusion.72
  255.2 75.5 %reduce-scatter.12.cloned.1.call-done = f32[2,128,256]{1,2,0:T(8,128)} async-done(((f32[2,1024,256]{1,2,0:T(8,128)}), f32[2,128,256]{1,2,0:T(8,128)}) %reduce-scatter.12.cloned.1.call-update) | async-done | bytes 262160 | tf_op jit(solution)/shard_map/reduce_scatter | solution.py:287
  332.8 1.5 convolution_add_fusion.1
  334.3 67.3 %reduce-scatter.14.cloned.1.call-done = f32[2,128,256]{2,1,0:T(8,128)} async-done(((f32[2,1024,256]{2,1,0:T(8,128)}), f32[2,128,256]{2,1,0:T(8,128)}) %reduce-scatter.14.cloned.1.call-update) | async-done | bytes 262160 | tf_op jit(solution)/shard_map/reduce_scatter | solution.py:288
  402.6 2.4 convolution_add_fusion
  405.0 1.8 fusion.50
  406.9 1.9 fusion.46
  411.7 5.1 convolution_bitcast_fusion.1
  416.7 9.8 copy.106
  428.0 5.1 fusion.75
  434.4 5.1 fusion.74
  441.4 41.7 %all-reduce.2 = (f32[64]{0:T(128)}, f32[64]{0:T(128)}) all-reduce(f32[64]{0:T(128)S(1)} %copy-done.47, f32[64]{0:T(128)S(1)} %copy-done.48), channel_id=1, replica_groups=mesh['ctx'=8,'seq'=2,'tp'=2] {'ctx','seq','tp'}, use_global_device_ids=true, to_apply=%region_36.37 | all-reduce | flops 128 | bytes 1024 | tf_op jit(solution)/shard_map/psum | solution.py:347
  483.1 2.4 add.233
  485.6 1.5 fusion.41
  487.1 40.5 %all-reduce.3 = (f32[1024]{0:T(1024)S(1)}, f32[1024]{0:T(1024)S(1)}) all-reduce(f32[1024]{0:T(1024)S(1)} %get-tuple-element.700, f32[1024]{0:T(1024)S(1)} %copy-done.39), channel_id=11, replica_groups=mesh['ctx'=8,'seq'=2,'tp'=2] {'ctx','seq'}, use_global_device_ids=true, to_apply=%region_32.33.clone | all-reduce | flops 2048 | bytes 16384
  528.8 2.8 fusion.38
  531.6 60.7 %reduce-scatter.16.cloned.1.call-done = f32[64,512]{1,0:T(8,128)} async-done(((f32[1024,512]{1,0:T(8,128)}), f32[64,512]{1,0:T(8,128)}) %reduce-scatter.16.cloned.1.call-update) | async-done | bytes 131088 | tf_op jit(solution)/shard_map/reduce_scatter | solution.py:337
  592.4 78.6 %reduce-scatter.18.cloned.1.call-done = f32[64,256]{1,0:T(8,128)} async-done(((f32[1024,256]{1,0:T(8,128)}), f32[64,256]{1,0:T(8,128)}) %reduce-scatter.18.cloned.1.call-update) | async-done | bytes 65552 | tf_op jit(solution)/shard_map/reduce_scatter | solution.py:338
  671.0 77.7 %reduce-scatter.20.cloned.1.call-done = f32[64,256]{1,0:T(8,128)} async-done(((f32[1024,256]{1,0:T(8,128)}), f32[64,256]{1,0:T(8,128)}) %reduce-scatter.20.cloned.1.call-update) | async-done | bytes 65552 | tf_op jit(solution)/shard_map/reduce_scatter | solution.py:339
  748.8 174.3 %reduce-scatter.28.cloned.1.call-done = f32[64,2304]{1,0:T(8,128)} async-done(((f32[1024,2304]{1,0:T(8,128)}), f32[64,2304]{1,0:T(8,128)}) %reduce-scatter.28.cloned.1.call-update) | async-done | bytes 589840
  923.1 176.9 %reduce-scatter.26.cloned.1.call-done = f32[64,2304]{1,0:T(8,128)} async-done(((f32[1024,2304]{1,0:T(8,128)}), f32[64,2304]{1,0:T(8,128)}) %reduce-scatter.26.cloned.1.call-update) | async-done | bytes 589840 | tf_op jit(solution)/shard_map/reduce_scatter | solution.py:342
  1100.0 177.0 %reduce-scatter.24.cloned.1.call-done = f32[64,2304]{1,0:T(8,128)} async-done(((f32[1024,2304]{1,0:T(8,128)}), f32[64,2304]{1,0:T(8,128)}) %reduce-scatter.24.cloned.1.call-update) | async-done | bytes 589840 | tf_op jit(solution)/shard_map/reduce_scatter | solution.py:341
  (220 shorter events, 44.5 us)
Async XLA Ops:
  7.2 77.5 %copy-start = (bf16[1024,512]{1,0:T(8,128)(2,1)S(1)}, bf16[1024,512]{1,0:T(8,128)(2,1)}, u32[]{:S(2)}) copy-start(bf16[1024,512]{1,0:T(8,128)(2,1)} %param.29) | copy-start | bytes 3145732
  7.2 7.4 copy-start.46
  7.2 8.2 copy-start.44
  7.2 62.4 %all-gather.4.cloned.1.call-start = ((), (), s32[]{:S(2)}) async-start(), calls=%async_computation.9 | async-start | bytes 2359296 | tf_op jit(solution)/shard_map/all_gather | solution.py:175
  7.3 9.8 copy-start.18
  9.9 8.5 copy-start.10
  12.8 7.3 copy-start.27
  14.2 6.0 copy-start.42
  15.4 4.9 copy-start.33
  15.4 4.9 copy-start.35
  15.6 5.4 copy-start.28
  16.4 87.6 %all-reduce.9.cloned.1.call-start = ((), (), s32[]{:S(2)}) async-start(), calls=%async_computation.10 | async-start | bytes 2097152 | tf_op jit(solution)/shard_map/psum | solution.py:200
  83.6 20.4 %copy-start.6 = (bf16[2,128,1024]{2,1,0:T(8,128)(2,1)S(1)}, bf16[2,128,1024]{2,1,0:T(8,128)(2,1)}, u32[]{:S(2)}) copy-start(bf16[2,128,1024]{2,1,0:T(8,128)(2,1)} %param.20) | copy-start | bytes 1572868
  83.6 21.9 %copy-start.38 = (f32[1024]{0:T(1024)S(1)}, f32[1024]{0:T(1024)}, u32[]{:S(2)}) copy-start(f32[1024]{0:T(1024)} %param.23) | copy-start | bytes 12292
  84.7 14.2 %copy-start.20 = (bf16[2,128,4,2,64]{1,0,4,3,2:T(2,128)(2,1)}, bf16[2,128,4,2,64]{1,0,4,3,2:T(2,128)(2,1)S(1)}, u32[]{:S(2)}) copy-start(bf16[2,128,4,2,64]{1,0,4,3,2:T(2,128)(2,1)S(1)} %copy.82) | copy-start | bytes 786436
  86.2 53.0 %all-reduce.11.cloned.1.call-start = ((), (), s32[]{:S(2)}) async-start(), calls=%async_computation.11 | async-start | bytes 2097152 | tf_op jit(solution)/shard_map/psum | solution.py:223
  105.4 35.8 %copy-start.4 = (f32[256,1024]{1,0:T(8,128)}, f32[256,1024]{1,0:T(8,128)S(1)}, u32[]{:S(2)}) copy-start(f32[256,1024]{1,0:T(8,128)S(1)} %get-tuple-element.741) | copy-start | bytes 3145732
  105.4 4.6 slice-start
  105.6 5.9 slice-start.4
  110.1 5.9 slice-start.2
  118.4 63.9 %all-gather.8.cloned.1.call-start = ((), (), s32[]{:S(2)}) async-start(), calls=%async_computation.13 | async-start | bytes 1179648 | tf_op jit(solution)/shard_map/all_gather | solution.py:241
  119.0 104.2 %all-gather.6.cloned.1.call-start = ((), (), s32[]{:S(2)}) async-start(), calls=%async_computation.12 | async-start | bytes 1179648 | tf_op jit(solution)/shard_map/all_gather | solution.py:240
  119.5 211.3 %reduce-scatter.12.cloned.1.call-start = ((), (), s32[]{:S(2)}) async-start(), calls=%async_computation.14 | async-start | bytes 2359296 | tf_op jit(solution)/shard_map/reduce_scatter | solution.py:287
  236.3 5.9 copy-start.2
  245.0 156.6 %reduce-scatter.14.cloned.1.call-start = ((), (), s32[]{:S(2)}) async-start(), calls=%async_computation.15 | async-start | bytes 2359296 | tf_op jit(solution)/shard_map/reduce_scatter | solution.py:288
  246.9 236.2 %all-reduce.13.cloned.1.call-start = ((), (), s32[]{:S(2)}) async-start(), calls=%async_computation.23 | async-start | bytes 4194304 | tf_op jit(solution)/shard_map/psum | solution.py:209
  247.1 5.3 copy-start.34
  247.2 5.2 copy-start.36
  247.2 6.4 copy-start.15
  247.2 6.4 copy-start.43
  247.2 7.5 copy-start.19
  252.4 79.4 %copy-start.17 = (f32[2,128,4,64]{1,3,2,0:T(8,128)S(1)}, f32[2,128,4,64]{1,3,2,0:T(8,128)}, u32[]{:S(2)}) copy-start(f32[2,128,4,64]{1,3,2,0:T(8,128)} %copy-done.16) | copy-start | bytes 786436
  252.4 79.4 %copy-start.45 = (f32[64]{0:T(128)S(1)}, f32[64]{0:T(128)}, u32[]{:S(2)}) copy-start(f32[64]{0:T(128)} %param.25) | copy-start | bytes 772
  254.7 78.0 %copy-start.22 = (bf16[2,128,8,64]{1,0,3,2:T(2,128)(2,1)}, bf16[2,128,8,64]{1,0,3,2:T(2,128)(2,1)S(1)}, u32[]{:S(2)}) copy-start(bf16[2,128,8,64]{1,0,3,2:T(2,128)(2,1)S(1)} %copy.89) | copy-start | bytes 786436
  332.6 72.4 %copy-start.9 = (f32[256,1024]{1,0:T(8,128)S(1)}, f32[256,1024]{1,0:T(8,128)}, u32[]{:S(2)}) copy-start(f32[256,1024]{1,0:T(8,128)} %copy-done.8) | copy-start | bytes 3145732
  332.6 72.4 %copy-start.21 = (bf16[2,128,4,2,64]{1,0,4,3,2:T(2,128)(2,1)S(1)}, bf16[2,128,4,2,64]{1,0,4,3,2:T(2,128)(2,1)}, u32[]{:S(2)}) copy-start(bf16[2,128,4,2,64]{1,0,4,3,2:T(2,128)(2,1)} %copy-done.20) | copy-start | bytes 786436
  404.9 126.7 %reduce-scatter.22.cloned.1.call-start = ((), (), s32[]{:S(2)}) async-start(), calls=%async_computation.19 | async-start | bytes 2228224 | tf_op jit(solution)/shard_map/reduce_scatter | solution.py:340
  406.8 185.6 %reduce-scatter.16.cloned.1.call-start = ((), (), s32[]{:S(2)}) async-start(), calls=%async_computation.16 | async-start | bytes 2228224 | tf_op jit(solution)/shard_map/reduce_scatter | solution.py:337
  408.8 262.2 %reduce-scatter.18.cloned.1.call-start = ((), (), s32[]{:S(2)}) async-start(), calls=%async_computation.17 | async-start | bytes 1114112 | tf_op jit(solution)/shard_map/reduce_scatter | solution.py:338
  410.2 338.6 %reduce-scatter.20.cloned.1.call-start = ((), (), s32[]{:S(2)}) async-start(), calls=%async_computation.18 | async-start | bytes 1114112 | tf_op jit(solution)/shard_map/reduce_scatter | solution.py:339
  411.6 511.5 %reduce-scatter.28.cloned.1.call-start = ((), (), s32[]{:S(2)}) async-start(), calls=%async_computation.22 | async-start | bytes 10027008
  426.6 673.4 %reduce-scatter.26.cloned.1.call-start = ((), (), s32[]{:S(2)}) async-start(), calls=%async_computation.21 | async-start | bytes 10027008 | tf_op jit(solution)/shard_map/reduce_scatter | solution.py:342
  433.2 843.9 %reduce-scatter.24.cloned.1.call-start = ((), (), s32[]{:S(2)}) async-start(), calls=%async_computation.20 | async-start | bytes 10027008 | tf_op jit(solution)/shard_map/reduce_scatter | solution.py:341
  439.5 43.6 %copy-start.5 = (f32[256,1024]{1,0:T(8,128)S(1)}, f32[256,1024]{1,0:T(8,128)}, u32[]{:S(2)}) copy-start(f32[256,1024]{1,0:T(8,128)} %copy-done.4) | copy-start | bytes 3145732
  439.5 46.1 %copy-start.7 = (bf16[2,128,1024]{2,1,0:T(8,128)(2,1)S(1)}, bf16[2,128,1024]{2,1,0:T(8,128)(2,1)}, u32[]{:S(2)}) copy-start(bf16[2,128,1024]{2,1,0:T(8,128)(2,1)} %param.20) | copy-start | bytes 1572868
  439.5 46.0 %copy-start.37 = (f32[1024]{0:T(1024)S(1)}, f32[1024]{0:T(1024)}, u32[]{:S(2)}) copy-start(f32[1024]{0:T(1024)} %param.22) | copy-start | bytes 12292
  439.5 47.6 %copy-start.39 = (f32[1024]{0:T(1024)S(1)}, f32[1024]{0:T(1024)}, u32[]{:S(2)}) copy-start(f32[1024]{0:T(1024)} %get-tuple-element.698) | copy-start | bytes 12292
  483.1 793.9 %copy-start.1 = (bf16[1024,512]{1,0:T(8,128)(2,1)S(1)}, bf16[1024,512]{1,0:T(8,128)(2,1)}, u32[]{:S(2)}) copy-start(bf16[1024,512]{1,0:T(8,128)(2,1)} %param.29) | copy-start | bytes 3145732
  (23 other events, 44.2 us)
Sparse Core Ops, SparseCore 0:
  16.5 53.0 all-gather.3
  86.3 17.6 all-reduce.8
  118.5 20.5 all-reduce.10
  141.6 40.5 all-gather.7
  184.7 38.3 all-gather.5
  245.1 85.6 reduce-scatter.11
  334.3 67.2 reduce-scatter.13
  405.1 20.4 all-reduce.12
  428.5 82.8 reduce-scatter.21
  514.0 78.3 reduce-scatter.15
  595.2 75.7 reduce-scatter.17
  673.7 75.0 reduce-scatter.19
  755.0 167.9 reduce-scatter.27
  929.2 170.7 reduce-scatter.25
  1106.1 170.8 reduce-scatter.23
